TPU v7x, 128 devices: a whole 4x4x4 slice. The times are simulated.
128 devices in a mesh: dp: 4 (over y), dict: 32 (over x, z, core).
Axes of the slice: x: 4, y: 4, z: 4, core: 2. Of those that a mesh axis runs over, the one named last changes fastest.
Arguments:
- acts: bfloat16 [8192, 8192], P('dict', 'dp'), may hold values from -6 to 6
- lists: int32 [512, 2], P('dict'), may hold values from 0 to 31, all different within a row; in each aligned block of 16 rows (0 to 15, 16 to 31, ...) at most 2 rows name the same one
- w_enc: bfloat16 [8192, 32768], P('dp', 'dict'), may hold values from -0.0625 to 0.0625
- w_dec: bfloat16 [32768, 8192], P('dict', 'dp'), may hold values from -0.1875 to 0.1875
- b_enc: bfloat16 [32768], P('dict'), may hold values from -3 to 3
- b_dec: bfloat16 [8192], P('dp'), may hold values from -3 to 3
Outputs:
- grad_enc: bfloat16 [8192, 32768], P('dp', 'dict')
- grad_dec: bfloat16 [32768, 8192], P('dict', 'dp')
Inputs may be any that keep to these rules, and one draw needn't show every extreme that they name: Each row block lists 2 different panels. Among the 16 row blocks of one index of dict, no panel is listed by more than 2 blocks, and some panel is listed by exactly 2.
All inputs are finite; a program needn't handle non-finite values.
Results may differ from a plain program's by a relative error of at most 0.0057.
Values may be sent and summed in bfloat16 or wider, within the bound.
No kernel may reach another device: no remote copies, remote signals or barrier semaphores. Data moves between devices by JAX's collectives and lax.ppermute only.
A program may use at most 128 MiB of HBM per device.

v0:
```python
import jax
import jax.numpy as jnp
from jax import lax
from jax.sharding import PartitionSpec as P


def on_device(acts, lists, w_enc, w_dec, b_enc, b_dec):
    peers = lax.axis_size("dict")
    block_count = lists.shape[0]
    active_count = lists.shape[1]
    rows_block = acts.shape[0] // block_count
    feature_cols = acts.shape[1]
    capacity = max(2, (2 * block_count * active_count + peers - 1) // peers)
    slot_total = peers * capacity
    flat_ids = lists.reshape(-1)
    onehot = (flat_ids[:, None] == jnp.arange(peers, dtype=jnp.int32)[None, :]).astype(jnp.int32)
    rank_index = jnp.sum((jnp.cumsum(onehot, axis=0) - 1) * onehot, axis=1)
    slot_index = flat_ids * capacity + rank_index
    item_block = jnp.arange(block_count * active_count, dtype=jnp.int32) // active_count
    slot_match = (jnp.arange(slot_total, dtype=jnp.int32)[:, None] == slot_index[None, :]).astype(
        jnp.float32
    )
    block_match = (item_block[:, None] == jnp.arange(block_count, dtype=jnp.int32)[None, :]).astype(
        jnp.float32
    )
    selector = jnp.dot(slot_match, block_match).astype(jnp.bfloat16)
    block_rows = acts.reshape(block_count, rows_block * feature_cols)
    outgoing = jnp.dot(selector, block_rows, preferred_element_type=jnp.float32).astype(
        jnp.bfloat16
    )
    outgoing = outgoing.reshape(peers, capacity * rows_block, feature_cols)
    received = lax.all_to_all(outgoing, "dict", split_axis=0, concat_axis=0, tiled=True)
    rows_in = received.reshape(-1, feature_cols)
    pre_local = jnp.dot(rows_in, w_enc, preferred_element_type=jnp.float32)
    bias_enc = b_enc.astype(jnp.float32)
    preact = lax.psum(pre_local, "dp") + bias_enc
    activity = (jnp.maximum(preact, 0.0) ** 2).astype(jnp.bfloat16)
    part = jnp.dot(activity, w_dec, preferred_element_type=jnp.float32).astype(jnp.bfloat16)
    part = part.reshape(peers, capacity * rows_block, feature_cols)
    returned = lax.all_to_all(part, "dict", split_axis=0, concat_axis=0, tiled=True)
    returned = returned.reshape(slot_total, rows_block * feature_cols)
    rebuilt = lax.dot_general(
        selector, returned, (((0,), (0,)), ((), ())), preferred_element_type=jnp.float32
    )
    rebuilt = rebuilt.reshape(block_count * rows_block, feature_cols) + b_dec.astype(jnp.float32)
    residual_g = ((rebuilt - acts.astype(jnp.float32)) * (1.0 / rows_block)).astype(jnp.bfloat16)
    resid_out = jnp.dot(
        selector,
        residual_g.reshape(block_count, rows_block * feature_cols),
        preferred_element_type=jnp.float32,
    ).astype(jnp.bfloat16)
    resid_out = resid_out.reshape(peers, capacity * rows_block, feature_cols)
    residual_in = lax.all_to_all(
        resid_out, "dict", split_axis=0, concat_axis=0, tiled=True
    ).reshape(-1, feature_cols)
    grad_dec = lax.dot_general(
        activity, residual_in, (((0,), (0,)), ((), ())), preferred_element_type=jnp.float32
    ).astype(jnp.bfloat16)
    dact_local = lax.dot_general(
        residual_in, w_dec, (((1,), (1,)), ((), ())), preferred_element_type=jnp.float32
    )
    dact = lax.psum(dact_local, "dp")
    grad_pre = (dact * 2.0 * jnp.maximum(preact, 0.0)).astype(jnp.bfloat16)
    grad_enc = lax.dot_general(
        rows_in, grad_pre, (((0,), (0,)), ((), ())), preferred_element_type=jnp.float32
    ).astype(jnp.bfloat16)
    return (grad_enc, grad_dec)


def solution(mesh):
    in_specs = (
        P("dict", "dp"),
        P("dict", None),
        P("dp", "dict"),
        P("dict", "dp"),
        P("dict"),
        P("dp"),
    )
    out_specs = (P("dp", "dict"), P("dict", "dp"))
    return jax.shard_map(
        on_device, mesh=mesh, in_specs=in_specs, out_specs=out_specs, check_vma=False
    )
```

profile of v0, /device:TPU:1, one launch (start us, length us, event | category | flops | bytes accessed | tf_op | source)
XLA Modules:
  0.0 449.6 jit_solution(6548300190928002087)
XLA Ops:
  7.2 0.8 copy.9
  8.4 1.6 reshape.59
  10.2 3.3 convolution_convert_fusion.1
  13.5 7.4 %reshape.60 = bf16[32,32,2048]{2,1,0:T(8,128)(2,1)} reshape(bf16[64,32768]{1,0:T(8,128)(2,1)} %convolution_convert_fusion.1) | data formatting | bytes 8388608 | tf_op jit(solution)/shard_map/reshape | solution.py:31
  20.9 60.3 %all_to_all.15 = bf16[32,32,2048]{2,1,0:T(8,128)(2,1)S(1)} all-to-all(bf16[32,32,2048]{2,1,0:T(8,128)(2,1)} %reshape.60), channel_id=1, replica_groups=mesh['dp'=4,'dict'=32] {'dict'}, dimensions={0} | all-to-all | bytes 8388608 | tf_op jit(solution)/shard_map/all_to_all | solution.py:32
  81.2 2.0 copy-done
  83.1 6.0 %fusion.10 = f32[1024,1024]{1,0:T(8,128)} fusion(bf16[1024,2048]{1,0:T(8,128)(2,1)S(1)} %bitcast.16, bf16[2048,1024]{1,0:T(8,128)(2,1)S(1)} %copy-done.5), kind=kOutput, calls=%fused_computation.29 | convolution fusion | flops 4294967296 | bytes 12582912 | tf_op jit(solution)/shard_map/dot_general | solution.py:34
  89.8 89.8 %all-reduce.3.cloned.1.call-done = f32[1024,1024]{1,0:T(8,128)} async-done(((f32[1024,1024]{1,0:T(8,128)}), f32[1024,1024]{1,0:T(8,128)}) %all-reduce.3.cloned.1.call-update) | async-done | bytes 4194320 | tf_op jit(solution)/shard_map/psum | solution.py:36
  179.6 10.0 %convolution_convert_fusion.4 = bf16[1024,2048]{1,0:T(8,128)(2,1)} fusion(bf16[1024,2048]{1,0:T(8,128)(2,1)} %param.9, f32[1024,1024]{1,0:T(8,128)} %all-reduce.3.cloned.1.call-done, f32[1024]{0:T(1024)S(1)} %convert_element_type.44), kind=kOutput, calls=%fused_computation.7 | convolution fusion | flops 4301258752 | bytes 12587008 | tf_op jit(solution)/shard_map/dot_general | solution.py:38
  189.6 8.0 %all-to-all-start.1 = ((bf16[32,32,2048]{2,1,0:T(8,128)(2,1)}), bf16[32,32,2048]{2,1,0:T(8,128)(2,1)}, u32[]{:S(2)}, u32[]{:S(2)}) async-start(bf16[32,32,2048]{2,1,0:T(8,128)(2,1)} %bitcast.20), calls=%async_computation.1 | async-start | bytes 8388608 | tf_op jit(solution)/shard_map/all_to_all | solution.py:40
  197.7 52.0 %all-to-all-done.1 = bf16[32,32,2048]{2,1,0:T(8,128)(2,1)} async-done(((bf16[32,32,2048]{2,1,0:T(8,128)(2,1)}), bf16[32,32,2048]{2,1,0:T(8,128)(2,1)}, u32[]{:S(2)}, u32[]{:S(2)}) %all-to-all-start.1) | async-done | bytes 4194336 | tf_op jit(solution)/shard_map/all_to_all | solution.py:40
  249.7 7.4 %reshape.63 = bf16[64,32768]{1,0:T(8,128)(2,1)} reshape(bf16[32,32,2048]{2,1,0:T(8,128)(2,1)} %all-to-all-done.1) | data formatting | bytes 8388608 | tf_op jit(solution)/shard_map/reshape | solution.py:41
  257.1 4.3 fusion.11
  261.4 1.7 reshape.64
  263.1 1.3 multiply_convert_fusion.3
  264.5 1.6 reshape.65
  266.0 3.3 convolution_convert_fusion
  269.3 7.4 %reshape.66 = bf16[32,32,2048]{2,1,0:T(8,128)(2,1)} reshape(bf16[64,32768]{1,0:T(8,128)(2,1)} %convolution_convert_fusion) | data formatting | bytes 8388608 | tf_op jit(solution)/shard_map/reshape | solution.py:52
  276.7 57.9 %all_to_all.16 = bf16[32,32,2048]{2,1,0:T(8,128)(2,1)S(1)} all-to-all(bf16[32,32,2048]{2,1,0:T(8,128)(2,1)} %reshape.66), channel_id=1, replica_groups=mesh['dp'=4,'dict'=32] {'dict'}, dimensions={0} | all-to-all | bytes 8388608 | tf_op jit(solution)/shard_map/all_to_all | solution.py:53
  334.6 1.9 copy-done.1
  336.5 6.1 %fusion.12 = f32[1024,1024]{1,0:T(8,128)} fusion(bf16[1024,2048]{1,0:T(8,128)(2,1)S(1)} %bitcast.18, bf16[1024,2048]{1,0:T(8,128)(2,1)S(1)} %copy-done.6), kind=kOutput, calls=%fused_computation.31 | convolution fusion | flops 4294967296 | bytes 12582912 | tf_op jit(solution)/shard_map/dot_general | solution.py:59
  342.6 10.1 %convolution_convert_fusion.2 = bf16[1024,2048]{1,0:T(8,128)(2,1)} fusion(bf16[1024,2048]{1,0:T(8,128)(2,1)} %bitcast.19, f32[1024,1024]{1,0:T(8,128)} %all-reduce.3.cloned.1.call-done, f32[1024]{0:T(1024)S(1)} %convert_element_type.44), kind=kOutput, calls=%fused_computation.5 | convolution fusion | flops 4301258752 | bytes 12587008 | tf_op jit(solution)/shard_map/dot_general | solution.py:56
  352.7 78.8 %all-reduce.5.cloned.1.call-done = f32[1024,1024]{1,0:T(8,128)} async-done(((f32[1024,1024]{1,0:T(8,128)}), f32[1024,1024]{1,0:T(8,128)}) %all-reduce.5.cloned.1.call-update) | async-done | bytes 4194320 | tf_op jit(solution)/shard_map/psum | solution.py:62
  431.5 11.3 %convolution_convert_fusion.3 = bf16[2048,1024]{1,0:T(8,128)(2,1)} fusion(bf16[1024,2048]{1,0:T(8,128)(2,1)} %bitcast.17, f32[1024,1024]{1,0:T(8,128)} %all-reduce.5.cloned.1.call-done, f32[1024,1024]{1,0:T(8,128)} %all-reduce.3.cloned.1.call-done, f32[1024]{0:T(1024)S(1)} %convert_element_type.44), kind=kOutput, calls=%fused_computation.6 | convolution fusion | flops 4302307328 | bytes 16781312 | tf_op jit(solution)/shard_map/dot_general | solution.py:64
  (24 shorter events, 1.4 us)
Async XLA Ops:
  7.2 172.5 %all-reduce.3.cloned.1.call-start = ((), (), s32[]{:S(2)}) async-start(), calls=%async_computation.3 | async-start | bytes 8388608 | tf_op jit(solution)/shard_map/psum | solution.py:36
  20.9 62.3 %copy-start.5 = (bf16[2048,1024]{1,0:T(8,128)(2,1)S(1)}, bf16[2048,1024]{1,0:T(8,128)(2,1)}, u32[]{:S(2)}) copy-start(bf16[2048,1024]{1,0:T(8,128)(2,1)} %param.8) | copy-start | bytes 12582916
  81.2 2.0 copy-start
  89.1 0.7 copy-start.4
  189.6 8.1 %copy-start.3 = (bf16[2048]{0:T(1024)(128)(2,1)S(1)}, bf16[2048]{0:T(1024)(128)(2,1)}, u32[]{:S(2)}) copy-start(bf16[2048]{0:T(1024)(128)(2,1)} %param.11) | copy-start | bytes 12292
  189.6 60.1 %all-to-all-start.1 = ((bf16[32,32,2048]{2,1,0:T(8,128)(2,1)}), bf16[32,32,2048]{2,1,0:T(8,128)(2,1)}, u32[]{:S(2)}, u32[]{:S(2)}) async-start(bf16[32,32,2048]{2,1,0:T(8,128)(2,1)} %bitcast.20), calls=%async_computation.1 | async-start | bytes 8388608 | tf_op jit(solution)/shard_map/all_to_all | solution.py:40
  197.6 233.8 %all-reduce.5.cloned.1.call-start = ((), (), s32[]{:S(2)}) async-start(), calls=%async_computation.4 | async-start | bytes 8388608 | tf_op jit(solution)/shard_map/psum | solution.py:62
  257.1 6.0 %copy-start.2 = (bf16[256,2048]{1,0:T(8,128)(2,1)S(1)}, bf16[256,2048]{1,0:T(8,128)(2,1)}, u32[]{:S(2)}) copy-start(bf16[256,2048]{1,0:T(8,128)(2,1)} %param.6) | copy-start | bytes 3145732
  276.7 59.9 %copy-start.6 = (bf16[1024,2048]{1,0:T(8,128)(2,1)S(1)}, bf16[1024,2048]{1,0:T(8,128)(2,1)}, u32[]{:S(2)}) copy-start(bf16[1024,2048]{1,0:T(8,128)(2,1)} %param.9) | copy-start | bytes 12582916
  334.6 1.9 copy-start.1
Sparse Core Ops, SparseCore 0:
  89.3 90.3 all-reduce.2
  342.7 88.6 all-reduce.4
where the time goes:
time: 450 us
  waiting for transfers between devices  221 us (49%)
  blocking collectives  118 us (26%)
  matrix products  54.5 us (12%)
  local copies, waits for them, and re-layouts  32.4 us (7%)
  between operations  14.1 us (3%)
  starting transfers between devices  8.1 us (2%)
    psum x1, waiting for transfers between devices, on_device(): preact = lax.psum(pre_local, 'dp') + bias_enc  89.8 us
    psum x1, waiting for transfers between devices, on_device(): dact = lax.psum(dact_local, 'dp')  78.8 us
    all_to_all x1, blocking collectives, on_device(): lax.all_to_all(outgoing, 'dict', split_axis=0, concat_axis=0, tiled=True)  60.3 us
    all_to_all x1, blocking collectives, on_device(): lax.all_to_all(resid_out, 'dict', split_axis=0, concat_axis=0, tiled=True)  57.9 us
    all_to_all x1, waiting for transfers between devices, on_device(): lax.all_to_all(part, 'dict', split_axis=0, concat_axis=0, tiled=True)  52 us
    dot_general x1, matrix products, on_device(): lax.dot_general(rows_in, grad_pre, (((0,), (0,)), ((), ())), preferred_el...  11.3 us
    dot_general x1, matrix products, on_device(): lax.dot_general(activity, residual_in, (((0,), (0,)), ((), ())), preferre...  10.1 us
    dot_general x1, matrix products, on_device(): jnp.dot(activity, w_dec, preferred_element_type=jnp.float32)  9.98 us
  transfers between devices with their start and end apart: 3, of which 3 were waited for; matrix products, arithmetic and copies ran while one was open for 2% of the time, Pallas kernels for 0%

commit v1 on v0

--- a/solution.py
+++ b/solution.py
@@ -59,7 +59,7 @@
     dact_local = lax.dot_general(
         residual_in, w_dec, (((1,), (1,)), ((), ())), preferred_element_type=jnp.float32
     )
-    dact = lax.psum(dact_local, "dp")
+    dact = jnp.sum(lax.all_gather(dact_local, "dp"), axis=0)
     grad_pre = (dact * 2.0 * jnp.maximum(preact, 0.0)).astype(jnp.bfloat16)
     grad_enc = lax.dot_general(
         rows_in, grad_pre, (((0,), (0,)), ((), ())), preferred_element_type=jnp.float32

time: 450 us -> 522 us (1.16)
  waiting for transfers between devices: 221 us -> 282 us
  other arithmetic: 1.64 us -> 11.9 us
    all_gather x0 -> x1, waiting for transfers between devices: none -> 140 us  [on_device(): dact = jnp.sum(lax.all_gather(dact_local, 'dp'), axis=0)]
    psum x1 -> x0, waiting for transfers between devices: 78.8 us -> none  [on_device(): dact = lax.psum(dact_local, 'dp')]
    reduce_sum x0 -> x1, other arithmetic: none -> 10.3 us  [on_device(): dact = jnp.sum(lax.all_gather(dact_local, 'dp'), axis=0)]
where the time goes in v1:
time: 522 us; the launch traced here: 521 us
  waiting for transfers between devices  282 us (54%)
  blocking collectives  118 us (23%)
  matrix products  54.7 us (10%)
  local copies, waits for them, and re-layouts  32.4 us (6%)
  between operations  14.1 us (3%)
  other arithmetic  11.9 us (2%)
  starting transfers between devices  8.1 us (2%)
    all_gather x1, waiting for transfers between devices, on_device(): dact = jnp.sum(lax.all_gather(dact_local, 'dp'), axis=0)  140 us
    psum x1, waiting for transfers between devices, on_device(): preact = lax.psum(pre_local, 'dp') + bias_enc  89.8 us
    all_to_all x1, blocking collectives, on_device(): lax.all_to_all(outgoing, 'dict', split_axis=0, concat_axis=0, tiled=True)  60.3 us
    all_to_all x1, blocking collectives, on_device(): lax.all_to_all(resid_out, 'dict', split_axis=0, concat_axis=0, tiled=True)  57.9 us
    all_to_all x1, waiting for transfers between devices, on_device(): lax.all_to_all(part, 'dict', split_axis=0, concat_axis=0, tiled=True)  52 us
    dot_general x1, matrix products, on_device(): lax.dot_general(rows_in, grad_pre, (((0,), (0,)), ((), ())), preferred_el...  11.3 us
  transfers between devices with their start and end apart: 3, of which 3 were waited for; matrix products, arithmetic and copies ran while one was open for 2% of the time, Pallas kernels for 0%

profile of v1, /device:TPU:1, one launch (start us, length us, event | category | flops | bytes accessed | tf_op | source)
XLA Modules:
  0.0 521.2 jit_solution(18428496653221606276)
XLA Ops:
  8.4 1.6 reshape.59
  10.2 3.3 convolution_convert_fusion.1
  13.5 7.4 %reshape.60 = bf16[32,32,2048]{2,1,0:T(8,128)(2,1)} reshape(bf16[64,32768]{1,0:T(8,128)(2,1)} %convolution_convert_fusion.1) | data formatting | bytes 8388608 | tf_op jit(solution)/shard_map/reshape | solution.py:31
  20.9 60.3 %all_to_all.15 = bf16[32,32,2048]{2,1,0:T(8,128)(2,1)S(1)} all-to-all(bf16[32,32,2048]{2,1,0:T(8,128)(2,1)} %reshape.60), channel_id=1, replica_groups=mesh['dp'=4,'dict'=32] {'dict'}, dimensions={0} | all-to-all | bytes 8388608 | tf_op jit(solution)/shard_map/all_to_all | solution.py:32
  81.2 2.0 copy-done
  83.1 6.0 %fusion.10 = f32[1024,1024]{1,0:T(8,128)} fusion(bf16[1024,2048]{1,0:T(8,128)(2,1)S(1)} %bitcast.18, bf16[2048,1024]{1,0:T(8,128)(2,1)S(1)} %copy-done.5), kind=kOutput, calls=%fused_computation.29 | convolution fusion | flops 4294967296 | bytes 12582912 | tf_op jit(solution)/shard_map/dot_general | solution.py:34
  89.8 89.8 %all-reduce.2.cloned.1.call-done = f32[1024,1024]{1,0:T(8,128)} async-done(((f32[1024,1024]{1,0:T(8,128)}), f32[1024,1024]{1,0:T(8,128)}) %all-reduce.2.cloned.1.call-update) | async-done | bytes 4194320 | tf_op jit(solution)/shard_map/psum | solution.py:36
  179.6 10.0 %convolution_convert_fusion.4 = bf16[1024,2048]{1,0:T(8,128)(2,1)} fusion(bf16[1024,2048]{1,0:T(8,128)(2,1)} %param.9, f32[1024,1024]{1,0:T(8,128)} %all-reduce.2.cloned.1.call-done, f32[1024]{0:T(1024)S(1)} %convert_element_type.44), kind=kOutput, calls=%fused_computation.7 | convolution fusion | flops 4301258752 | bytes 12587008 | tf_op jit(solution)/shard_map/dot_general | solution.py:38
  189.6 8.0 %all-to-all-start.1 = ((bf16[32,32,2048]{2,1,0:T(8,128)(2,1)}), bf16[32,32,2048]{2,1,0:T(8,128)(2,1)}, u32[]{:S(2)}, u32[]{:S(2)}) async-start(bf16[32,32,2048]{2,1,0:T(8,128)(2,1)} %bitcast.22), calls=%async_computation.1 | async-start | bytes 8388608 | tf_op jit(solution)/shard_map/all_to_all | solution.py:40
  197.7 52.0 %all-to-all-done.1 = bf16[32,32,2048]{2,1,0:T(8,128)(2,1)} async-done(((bf16[32,32,2048]{2,1,0:T(8,128)(2,1)}), bf16[32,32,2048]{2,1,0:T(8,128)(2,1)}, u32[]{:S(2)}, u32[]{:S(2)}) %all-to-all-start.1) | async-done | bytes 4194336 | tf_op jit(solution)/shard_map/all_to_all | solution.py:40
  249.7 7.4 %reshape.63 = bf16[64,32768]{1,0:T(8,128)(2,1)} reshape(bf16[32,32,2048]{2,1,0:T(8,128)(2,1)} %all-to-all-done.1) | data formatting | bytes 8388608 | tf_op jit(solution)/shard_map/reshape | solution.py:41
  257.1 4.3 fusion.11
  261.4 1.7 reshape.64
  263.1 1.3 multiply_convert_fusion.3
  264.5 1.6 reshape.65
  266.0 3.3 convolution_convert_fusion
  269.3 7.4 %reshape.66 = bf16[32,32,2048]{2,1,0:T(8,128)(2,1)} reshape(bf16[64,32768]{1,0:T(8,128)(2,1)} %convolution_convert_fusion) | data formatting | bytes 8388608 | tf_op jit(solution)/shard_map/reshape | solution.py:52
  276.7 57.9 %all_to_all.16 = bf16[32,32,2048]{2,1,0:T(8,128)(2,1)S(1)} all-to-all(bf16[32,32,2048]{2,1,0:T(8,128)(2,1)} %reshape.66), channel_id=1, replica_groups=mesh['dp'=4,'dict'=32] {'dict'}, dimensions={0} | all-to-all | bytes 8388608 | tf_op jit(solution)/shard_map/all_to_all | solution.py:53
  334.6 1.9 copy-done.1
  336.5 6.1 %fusion.12 = f32[1024,1024]{1,0:T(8,128)} fusion(bf16[1024,2048]{1,0:T(8,128)(2,1)S(1)} %bitcast.20, bf16[1024,2048]{1,0:T(8,128)(2,1)S(1)} %copy-done.6), kind=kOutput, calls=%fused_computation.31 | convolution fusion | flops 4294967296 | bytes 12582912 | tf_op jit(solution)/shard_map/dot_general | solution.py:59
  342.6 10.3 %convolution_convert_fusion.2 = bf16[1024,2048]{1,0:T(8,128)(2,1)} fusion(bf16[1024,2048]{1,0:T(8,128)(2,1)} %bitcast.21, f32[1024,1024]{1,0:T(8,128)} %all-reduce.2.cloned.1.call-done, f32[1024]{0:T(1024)S(1)} %convert_element_type.44), kind=kOutput, calls=%fused_computation.5 | convolution fusion | flops 4301258752 | bytes 12587008 | tf_op jit(solution)/shard_map/dot_general | solution.py:56
  352.9 139.8 %all-gather.3.cloned.1.call-done = f32[4096,1024]{1,0:T(8,128)} async-done(((f32[1024,1024]{1,0:T(8,128)}), f32[4096,1024]{1,0:T(8,128)}) %all-gather.3.cloned.1.call-update) | async-done | bytes 16777232 | tf_op jit(solution)/shard_map/all_gather | solution.py:62
  492.7 10.3 %reduce_sum.19 = f32[1024,1024]{1,0:T(8,128)} reduce(f32[4,1024,1024]{2,1,0:T(8,128)} %bitcast.17, f32[]{:T(128)} %constant.29.clone.1), dimensions={0}, to_apply=%region_3.4 | reduce | flops 3145728 | bytes 20971524 | tf_op jit(solution)/shard_map/reduce_sum | solution.py:62
  503.0 11.3 %convolution_convert_fusion.3 = bf16[2048,1024]{1,0:T(8,128)(2,1)} fusion(bf16[1024,2048]{1,0:T(8,128)(2,1)} %bitcast.19, f32[1024,1024]{1,0:T(8,128)} %reduce_sum.19, f32[1024,1024]{1,0:T(8,128)} %all-reduce.2.cloned.1.call-done, f32[1024]{0:T(1024)S(1)} %convert_element_type.44), kind=kOutput, calls=%fused_computation.6 | convolution fusion | flops 4302307328 | bytes 16781312 | tf_op jit(solution)/shard_map/dot_general | solution.py:64
  (25 shorter events, 2.2 us)
Async XLA Ops:
  7.2 172.4 %all-reduce.2.cloned.1.call-start = ((), (), s32[]{:S(2)}) async-start(), calls=%async_computation.3 | async-start | bytes 8388608 | tf_op jit(solution)/shard_map/psum | solution.py:36
  20.9 62.3 %copy-start.5 = (bf16[2048,1024]{1,0:T(8,128)(2,1)S(1)}, bf16[2048,1024]{1,0:T(8,128)(2,1)}, u32[]{:S(2)}) copy-start(bf16[2048,1024]{1,0:T(8,128)(2,1)} %param.8) | copy-start | bytes 12582916
  81.2 2.0 copy-start
  89.1 0.7 copy-start.4
  189.6 8.1 %copy-start.3 = (bf16[2048]{0:T(1024)(128)(2,1)S(1)}, bf16[2048]{0:T(1024)(128)(2,1)}, u32[]{:S(2)}) copy-start(bf16[2048]{0:T(1024)(128)(2,1)} %param.11) | copy-start | bytes 12292
  189.6 60.1 %all-to-all-start.1 = ((bf16[32,32,2048]{2,1,0:T(8,128)(2,1)}), bf16[32,32,2048]{2,1,0:T(8,128)(2,1)}, u32[]{:S(2)}, u32[]{:S(2)}) async-start(bf16[32,32,2048]{2,1,0:T(8,128)(2,1)} %bitcast.22), calls=%async_computation.1 | async-start | bytes 8388608 | tf_op jit(solution)/shard_map/all_to_all | solution.py:40
  197.6 295.1 %all-gather.3.cloned.1.call-start = ((), (), s32[]{:S(2)}) async-start(), calls=%async_computation.4 | async-start | bytes 20971520 | tf_op jit(solution)/shard_map/all_gather | solution.py:62
  257.1 6.0 %copy-start.2 = (bf16[256,2048]{1,0:T(8,128)(2,1)S(1)}, bf16[256,2048]{1,0:T(8,128)(2,1)}, u32[]{:S(2)}) copy-start(bf16[256,2048]{1,0:T(8,128)(2,1)} %param.6) | copy-start | bytes 3145732
  276.7 59.9 %copy-start.6 = (bf16[1024,2048]{1,0:T(8,128)(2,1)S(1)}, bf16[1024,2048]{1,0:T(8,128)(2,1)}, u32[]{:S(2)}) copy-start(bf16[1024,2048]{1,0:T(8,128)(2,1)} %param.9) | copy-start | bytes 12582916
  334.6 1.9 copy-start.1
Sparse Core Ops, SparseCore 0:
  89.3 90.3 all-reduce.1
  342.7 149.9 all-gather.2
